TPU v7x, 512 devices: a whole 4x4x16 slice. The times are simulated.
512 devices in a mesh: coef: 16 (over z_lo, y), pair: 32 (over z_hi, x, core).
Axes of the slice: x: 4, y: 4, z: 16 (z_hi: 4, z_lo: 4; z = z_hi * 4 + z_lo), core: 2. Of those that a mesh axis runs over, the one named last changes fastest.
Arguments:
- integrals: bfloat16 [2048, 32, 8192], P(('coef', 'pair')), may hold values from -66 to 66
- coefficients: bfloat16 [2, 8192, 384], P(None, ('coef', 'pair')), may hold values from -0.0625 to 0.0625
- shell_starts: int32 [8], replicated, may hold values from 0 to 8188, as said below
- pair_ids: int32 [16, 128], P('coef'), may hold values from 0 to 127, each once within a row
Outputs:
- half_ints: bfloat16 [2, 384, 384, 2048], P(None, 'pair', None, 'coef')
Inputs may be any that keep to these rules, and one draw needn't show every extreme that they name: `shell_starts`: distinct multiples of 4.
All inputs are finite; a program needn't handle non-finite values.
Results may differ from a plain program's by a relative error of at most 0.0049.
Values may be sent and summed in bfloat16 or wider, within the bound.
A program may use at most 64 MiB of HBM per device.

v0:
```python
import jax
import jax.numpy as jnp
from jax import lax
from jax.sharding import PartitionSpec as P

SHW = 4


def on_device(integrals, coefficients, shell_starts, pair_ids):
    slot_count, batch_rows, ao_width = integrals.shape
    occupied = coefficients.shape[2]
    flat_ints = integrals.reshape(slot_count * batch_rows, ao_width)
    offsets = jnp.arange(SHW, dtype=jnp.int32)
    batch_index = (shell_starts[:, None] + offsets[None, :]).reshape(-1)
    panel_piece = lax.all_gather(coefficients, ("coef", "pair"), axis=1, tiled=True)
    products = jnp.einsum("rn,cnj->crj", flat_ints, panel_piece, preferred_element_type=jnp.float32)
    row_count = panel_piece.shape[1]
    inside_mask = (batch_index >= 0) & (batch_index < row_count)
    safe_index = jnp.clip(batch_index, 0, row_count - 1)
    chosen = jnp.take(panel_piece, safe_index, axis=1).astype(jnp.float32)
    picked = jnp.where(inside_mask[None, :, None], chosen, 0.0)
    half_done, picked = (products, picked)
    batch_coef = picked.astype(jnp.bfloat16)
    half_done = half_done.astype(jnp.bfloat16).reshape(2, slot_count, batch_rows, occupied)
    real_part = jnp.einsum(
        "mi,kmj->kij", batch_coef[0], half_done[0], preferred_element_type=jnp.float32
    ) + jnp.einsum("mi,kmj->kij", batch_coef[1], half_done[1], preferred_element_type=jnp.float32)
    imag_part = jnp.einsum(
        "mi,kmj->kij", batch_coef[0], half_done[1], preferred_element_type=jnp.float32
    ) - jnp.einsum("mi,kmj->kij", batch_coef[1], half_done[0], preferred_element_type=jnp.float32)
    local_block = jnp.stack([real_part, imag_part]).astype(jnp.bfloat16)
    arrived = lax.all_to_all(local_block, "pair", split_axis=2, concat_axis=1, tiled=True)
    pair_order = pair_ids.reshape(-1)
    columns = jnp.arange(pair_order.shape[0], dtype=jnp.int32)
    selector = (pair_order[:, None] == columns[None, :]).astype(jnp.bfloat16)
    result = jnp.einsum("csij,sq->cijq", arrived, selector, preferred_element_type=jnp.float32)
    return result.astype(jnp.bfloat16)


def solution(mesh):
    return jax.shard_map(
        on_device,
        mesh=mesh,
        in_specs=(
            P(("coef", "pair"), None, None),
            P(None, ("coef", "pair"), None),
            P(),
            P("coef", None),
        ),
        out_specs=P(None, "pair", None, "coef"),
        check_vma=False,
    )
```

profile of v0, /device:TPU:1, one launch (start us, length us, event | category | flops | bytes accessed | tf_op | source)
XLA Modules:
  0.0 1116.3 jit_solution(15795770854735174628)
XLA Ops:
  6.5 0.0 copy-start
  6.5 0.0 all-gather.2.cloned.1.call-start
  6.5 0.7 all-gather.2.cloned.1.call-update
  7.3 0.7 fusion.14
  8.0 0.1 min.18
  8.1 0.1 min.16
  8.1 0.7 fusion.17
  8.9 0.1 and.18
  9.0 835.0 %all-gather.2.cloned.1.call-done = bf16[2,8192,384]{2,1,0:T(8,128)(2,1)} async-done(((bf16[2,16,384]{2,1,0:T(8,128)(2,1)}), bf16[2,8192,384]{2,1,0:T(8,128)(2,1)}) %all-gather.2.cloned.1.call-update) | async-done | bytes 12582928 | tf_op jit(solution)/shard_map/all_gather | solution.py:15
  844.0 0.0 copy-done
  844.0 0.0 copy-start.1
  844.0 6.5 fusion.7
  850.6 1.6 copy-done.1
  852.2 117.8 %copy.11 = bf16[2,8192,384]{2,0,1:T(2,128)(2,1)} copy(bf16[2,8192,384]{2,1,0:T(8,128)(2,1)S(1)} %copy-done.1) | data formatting | bytes 25165824 | tf_op jit(solution)/shard_map/all_gather | solution.py:15
  970.0 5.2 gather_fusion
  975.2 0.1 fusion.10
  975.3 0.5 fusion.13
  975.8 0.5 fusion.12
  976.3 0.5 fusion.5
  976.8 0.5 fusion.6
  977.4 1.7 pad_maximum_fusion
  979.0 5.4 copy.13
  984.4 120.9 %all_to_all.18 = bf16[2,4,384,384]{3,1,0,2:T(4,128)(2,1)S(1)} all-to-all(bf16[2,4,384,384]{3,1,0,2:T(4,128)(2,1)} %copy.13), channel_id=1, replica_groups=mesh['coef'=16,'pair'=32] {'pair'}, dimensions={2} | all-to-all | bytes 4718592 | tf_op jit(solution)/shard_map/all_to_all | solution.py:32
  1105.3 0.0 copy-start.2
  1105.3 1.8 copy.15
  1107.1 0.0 copy-done.2
  1107.2 2.3 fusion.2
  (4 shorter events, 0.0 us)
Async XLA Ops:
  6.5 837.5 %copy-start = (bf16[4,32,8192]{2,1,0:T(8,128)(2,1)S(1)}, bf16[4,32,8192]{2,1,0:T(8,128)(2,1)}, u32[]{:S(2)}) copy-start(bf16[4,32,8192]{2,1,0:T(8,128)(2,1)} %param.4) | copy-start | bytes 6291460
  6.5 837.5 %all-gather.2.cloned.1.call-start = ((), (), s32[]{:S(2)}) async-start(), calls=%async_computation.1 | async-start | bytes 12607488 | tf_op jit(solution)/shard_map/all_gather | solution.py:15
  844.0 8.2 copy-start.1
  1105.3 1.8 copy-start.2
Sparse Core Ops, SparseCore 0:
  9.5 834.5 all-gather.1
where the time goes:
time: 1120 us
  waiting for transfers between devices  836 us (75%)
  local copies, waits for them, and re-layouts  132 us (12%)
  blocking collectives  121 us (11%)
  between operations  13.5 us (1%)
    all_gather x1, waiting for transfers between devices, on_device(): lax.all_gather(coefficients, ('coef', 'pair'), axis=1, tiled=True)  835 us
    all_to_all x1, blocking collectives, on_device(): lax.all_to_all(local_block, 'pair', split_axis=2, concat_axis=1, tiled=True)  121 us
    all_gather x1, local copies, waits for them, and re-layouts, on_device(): lax.all_gather(coefficients, ('coef', 'pair'), axis=1, tiled=True)  118 us
  transfers between devices with their start and end apart: 1, of which 1 were waited for; matrix products, arithmetic and copies ran while one was open for 0% of the time, Pallas kernels for 0%

commit v1 on v0

v1 whole, which is shorter than its diff:
```python
import jax
import jax.numpy as jnp
from jax import lax
from jax.experimental import pallas as pl
from jax.experimental.pallas import tpu as pltpu
from jax.sharding import PartitionSpec as P

MESH = pl.DeviceIdType.MESH
SHW = 4
F32 = jnp.float32
BF16 = jnp.bfloat16


def kernel(starts_ref, order_ref, ints_ref, coef_ref, out_ref,
           rows, panel, half, batch, mix, trans, outv,
           loc_sem, cc_s, cc_r, ci_s, ci_r, ring_s, ring_r, fx_s, fx_r, fy_s, fy_r, fz_s, fz_r,
           mid_s, mid_r, midf_s, midf_r, last_s, last_r, lastf_s, lastf_r,
           b_s, b_r, hz_s, hz_r, hzf_s, hzf_r, hx_s, hx_r, hxf_s, hxf_r, hp_s, hp_r):
    a = lax.axis_index("coef")
    p = lax.axis_index("pair")
    zlo, y = a // 4, a % 4
    zhi, x, c = p // 8, (p // 2) % 4, p % 2
    z = zhi * 4 + zlo
    other = 1 - c

    def dev(z_, y_, x_, c_):
        return ((z_ % 4) * 4 + y_, (z_ // 4) * 8 + x_ * 2 + c_)

    def zz(k):
        return (z + k + 16) % 16

    def yy(k):
        return (y + k + 4) % 4

    def xx(k):
        return (x + k + 4) % 4

    def hh(k):
        return (zhi + k + 4) % 4

    partner = dev(z, y, x, other)
    z_to = (dev(zz(1), y, x, c), dev(zz(-1), y, x, c))
    y_to = (dev(z, yy(1), x, c), dev(z, yy(-1), x, c))
    x_to = (dev(z, y, xx(1), c), dev(z, y, xx(-1), c))
    h_to = (dev(zz(4), y, x, c), dev(zz(-4), y, x, c))
    y_far = dev(z, yy(2), x, c)
    x_far = dev(z, y, xx(2), c)
    SIGN = (1, -1)

    def remote(ref, ssem, rsem, to):
        return pltpu.make_async_remote_copy(src_ref=ref, dst_ref=ref, send_sem=ssem, recv_sem=rsem,
                                            device_id=to, device_id_type=MESH)

    core_rows = pl.ds(pl.multiple_of(c * 16, 16), 16)
    int_rows = pl.ds(pl.multiple_of(c * 128, 128), 128)

    def own_coef(j):
        return pltpu.make_async_copy(coef_ref.at[c, :, pl.ds(128 * j, 128)],
                                     panel.at[j, zlo, y, zhi, x, core_rows, :], loc_sem.at[j])

    own_ints = pltpu.make_async_copy(ints_ref, rows.at[int_rows, :], loc_sem.at[3])

    def give_coef(j):
        return pltpu.make_async_remote_copy(
            src_ref=coef_ref.at[other, :, pl.ds(128 * j, 128)],
            dst_ref=panel.at[j, zlo, y, zhi, x, core_rows, :],
            send_sem=cc_s.at[j], recv_sem=cc_r.at[j], device_id=partner, device_id_type=MESH)

    def got_coef(j):
        ref = panel.at[j, zlo, y, zhi, x, pl.ds(pl.multiple_of(other * 16, 16), 16), :]
        return remote(ref, cc_s.at[j], cc_r.at[j], partner)

    give_ints = pltpu.make_async_remote_copy(
        src_ref=ints_ref, dst_ref=rows.at[int_rows, :],
        send_sem=ci_s.at[0], recv_sem=ci_r.at[0], device_id=partner, device_id_type=MESH)
    got_ints = remote(rows.at[pl.ds(pl.multiple_of(other * 128, 128), 128), :], ci_s.at[0], ci_r.at[0], partner)

    for j in (2, 0, 1):
        own_coef(j).start()
    own_ints.start()

    barrier = pltpu.get_barrier_semaphore()
    peers = (partner,) + z_to + y_to + x_to + h_to + (y_far, x_far)
    for peer in peers:
        pl.semaphore_signal(barrier, inc=1, device_id=peer, device_id_type=MESH)
    pl.semaphore_wait(barrier, len(peers))

    for j in (2, 0, 1):
        give_coef(j).start()
    give_ints.start()

    def ring(n, d, j, back):
        o = (z - SIGN[n] * (d - back) + 32) % 16
        return remote(panel.at[j, o % 4, y, o // 4, x], ring_s.at[n, d, j], ring_r.at[n, d, j], z_to[n])

    def fanx(k, back):
        to = (x_to[0], x_far, x_to[1])[k - 1]
        return remote(panel.at[2, zlo, y, zhi, xx(-k * (1 - back))], fx_s.at[k], fx_r.at[k], to)

    def fany(k, back):
        to = (y_to[0], y_far, y_to[1])[k - 1]
        return remote(panel.at[2, zlo, yy(-k * (1 - back)), zhi], fy_s.at[k], fy_r.at[k], to)

    def fanz(n, d, w, back):
        o = (z - SIGN[n] * (d - back) + 32) % 16
        return remote(panel.at[2, o % 4, w, o // 4], fz_s.at[n, d, w], fz_r.at[n, d, w], z_to[n])

    def ring_step(d, final=False):
        for n in range(2):
            for j in range(2):
                ring(n, d, j, 0).wait_recv()
                if not final or n == j:
                    ring(n, d + 1, j, 1).start()

    def fanz_step(d, final=False):
        for w in range(4):
            for n in range(2):
                fanz(n, d, w, 0).wait_recv()
                if not final or n == w // 2:
                    fanz(n, d + 1, w, 1).start()

    for j in (2, 0, 1):
        own_coef(j).wait()
        got_coef(j).wait_recv()
        if j == 2:
            for k in (1, 3, 2):
                fanx(k, 1).start()
        else:
            for n in range(2):
                ring(n, 1, j, 1).start()

    lane = lax.broadcasted_iota(jnp.int32, (32, 512), 1)
    row = lax.broadcasted_iota(jnp.int32, (32, 512), 0)
    want = row % SHW
    for s in range(8):
        want = want + jnp.where(row // SHW == s, starts_ref[s], 0)

    def pick(q, carry):
        at = pl.multiple_of(q * 512, 512)
        rows[256:288, pl.ds(at, 512)] = jnp.where(lane + q * 512 == want, 1.0, 0.0).astype(BF16)
        return carry

    ring_step(1)
    for k in (1, 3, 2):
        fanx(k, 0).wait_recv()
    for k in (1, 3, 2):
        fany(k, 1).start()
    lax.fori_loop(0, 16, pick, 0)
    ring_step(2)
    ring_step(3)

    def more(d, carry):
        ring_step(d)
        return carry

    lax.fori_loop(4, 7, more, 0)
    ring_step(7, True)
    for k in (1, 3, 2):
        fany(k, 0).wait_recv()
    for w in range(4):
        for n in range(2):
            fanz(n, 1, w, 1).start()
    for n in range(2):
        ring(n, 8, n, 0).wait_recv()

    def spot(ch, m, l):
        return (l, m) if ch == 0 else (m, l)

    mid_to = (x_to, y_to)
    last_to = (y_to, x_to)
    here = (x, y)
    line = (y, x)

    def wrap(v, k):
        return (v + k + 4) % 4

    def mid(ch, n, back):
        y_, x_ = spot(ch, wrap(here[ch], -SIGN[n] * (1 - back)), line[ch])
        return remote(panel.at[ch, :, y_, :, x_], mid_s.at[ch, n], mid_r.at[ch, n], mid_to[ch][n])

    def midf(ch, n, back):
        y_, x_ = spot(ch, wrap(here[ch], -SIGN[n] * (2 - back)), line[ch])
        return remote(panel.at[ch, pl.ds(2 * n, 2), y_, :, x_], midf_s.at[ch, n], midf_r.at[ch, n], mid_to[ch][n])

    def last(ch, k, n, back):
        y_, x_ = spot(ch, wrap(here[ch], k), wrap(line[ch], -SIGN[n] * (1 - back)))
        return remote(panel.at[ch, :, y_, :, x_], last_s.at[ch, k, n], last_r.at[ch, k, n], last_to[ch][n])

    def lastf(ch, k, n, back):
        y_, x_ = spot(ch, wrap(here[ch], k), wrap(line[ch], -SIGN[n] * (2 - back)))
        return remote(panel.at[ch, pl.ds(2 * n, 2), y_, :, x_], lastf_s.at[ch, k, n], lastf_r.at[ch, k, n],
                      last_to[ch][n])

    def last_go(k):
        for ch in range(2):
            for n in range(2):
                last(ch, k, n, 1).start()

    def last_on(k):
        for ch in range(2):
            for n in range(2):
                last(ch, k, n, 0).wait_recv()
                lastf(ch, k, n, 1).start()

    for ch in range(2):
        for n in range(2):
            mid(ch, n, 1).start()
    last_go(0)
    fanz_step(1)
    for ch in range(2):
        for n in range(2):
            mid(ch, n, 0).wait_recv()
            midf(ch, n, 1).start()
    last_go(1)
    last_go(3)
    fanz_step(2)
    for ch in range(2):
        for n in range(2):
            midf(ch, n, 0).wait_recv()
    last_go(2)
    fanz_step(3)
    last_on(0)
    fanz_step(4)
    last_on(1)
    fanz_step(5)
    last_on(3)
    fanz_step(6)
    last_on(2)
    fanz_step(7, True)
    own_ints.wait()
    got_ints.wait_recv()
    for w in range(4):
        fanz(w // 2, 8, w, 0).wait_recv()

    def piece(j, c_, x_, h_):
        return half.at[j, c_, x_, h_]

    def part(j, c_, x_, h_, n):
        return half.at[j, c_, x_, h_, pl.ds(128 * n, 128), :]

    def hz(j, n, back):
        return remote(piece(j, c, x, hh(-SIGN[n] * (1 - back))), hz_s.at[j, n], hz_r.at[j, n], h_to[n])

    def hzf(j, n, back):
        return remote(part(j, c, x, hh(-SIGN[n] * (2 - back)), n), hzf_s.at[j, n], hzf_r.at[j, n], h_to[n])

    def hx(j, k, n, back):
        return remote(piece(j, c, xx(-SIGN[n] * (1 - back)), hh(k)), hx_s.at[j, k, n], hx_r.at[j, k, n], x_to[n])

    def hxf(j, k, n, back):
        return remote(part(j, c, xx(-SIGN[n] * (2 - back)), hh(k), n), hxf_s.at[j, k, n], hxf_r.at[j, k, n], x_to[n])

    def hp(j, xk, k, c_):
        return remote(piece(j, c_, xx(xk), hh(k)), hp_s.at[j, xk, k], hp_r.at[j, xk, k], partner)

    def contract(j):
        def step(q, acc):
            at = pl.multiple_of(q * 512, 512)
            block = panel[j, q // 4, q % 4].reshape(512, 128)
            return acc + jnp.dot(rows[:, pl.ds(at, 512)], block, preferred_element_type=F32)

        acc = lax.fori_loop(0, 16, step, jnp.zeros((288, 128), F32))
        half[j, c, x, zhi] = acc[:256].astype(BF16)
        batch[c, :, 128 * j:128 * (j + 1)] = acc[256:].astype(BF16)

    def spread(j, k):
        for n in range(2):
            hx(j, k, n, 1).start()
        hp(j, 0, k, c).start()

    def e0(j):
        for n in range(2):
            hz(j, n, 1).start()
        spread(j, 0)

    def e1(j):
        for n in range(2):
            hz(j, n, 0).wait_recv()
            hzf(j, n, 1).start()
        spread(j, 1)
        spread(j, 3)

    def e2(j):
        for n in range(2):
            hzf(j, n, 0).wait_recv()
        spread(j, 2)

    def x1(j, k):
        for n in range(2):
            hx(j, k, n, 0).wait_recv()
            hxf(j, k, n, 1).start()
        hp(j, 3, k, c).start()
        hp(j, 1, k, c).start()

    def x2(j, k):
        for n in range(2):
            hxf(j, k, n, 0).wait_recv()
        hp(j, 2, k, c).start()

    contract(2)
    e0(2)
    for k in (0, 1, 3, 2):
        for ch in range(2):
            for n in range(2):
                lastf(ch, k, n, 0).wait_recv()
    contract(0)
    e0(0)
    contract(1)
    e0(1)
    swap = remote(batch.at[c], b_s.at[0], b_r.at[0], partner)
    swap.start()

    J = (2, 0, 1)
    for j in J:
        x1(j, 0)
    remote(batch.at[other], b_s.at[0], b_r.at[0], partner).wait_recv()

    r96 = lax.broadcasted_iota(jnp.int32, (96, 384), 0)
    c384 = lax.broadcasted_iota(jnp.int32, (96, 384), 1)
    chosen = jnp.where(c384 == p * 12 + r96 // 8, 1.0, 0.0).astype(BF16)
    r256 = lax.broadcasted_iota(jnp.int32, (96, 256), 0)
    c256 = lax.broadcasted_iota(jnp.int32, (96, 256), 1)
    same = r256 % 8 == c256 // 32
    grid = []
    for t in range(2):
        wide = jnp.concatenate([batch[t]] * 8, axis=0)
        g = lax.dot_general(chosen, wide, (((1,), (1,)), ((), ())), preferred_element_type=F32)
        grid.append(jnp.where(same, g, 0.0))
    mix[0:96, 0:256] = grid[0].astype(BF16)
    mix[0:96, 256:512] = grid[1].astype(BF16)
    mix[96:192, 0:256] = (-grid[1]).astype(BF16)
    mix[96:192, 256:512] = grid[0].astype(BF16)
    spots = lax.broadcasted_iota(jnp.int32, (128, 128), 0)
    select = jnp.transpose(jnp.where(spots == order_ref[0:1, :], 1.0, 0.0)).astype(BF16)

    for j in J:
        x2(j, 0)
    e1(2)
    for k in (1, 3):
        x1(2, k)
    e1(0)
    for k in (1, 3):
        x2(2, k)
    for k in (1, 3):
        x1(0, k)
    e1(1)
    for k in (1, 3):
        x2(0, k)
    for k in (1, 3):
        x1(1, k)
    e2(2)
    for k in (1, 3):
        x2(1, k)
    x1(2, 2)
    e2(0)
    x2(2, 2)
    x1(0, 2)
    e2(1)
    x2(0, 2)
    x1(1, 2)
    x2(1, 2)

    def mixed(j):
        for xk in range(4):
            for k in range(4):
                hp(j, xk, k, other).wait_recv()

        def one(t, carry):
            h_, x_ = t // 4, t % 4
            v = jnp.dot(mix[:, 0:256], half[j, 0, x_, h_], preferred_element_type=F32)
            v = v + jnp.dot(mix[:, 256:512], half[j, 1, x_, h_], preferred_element_type=F32)
            trans[:, pl.ds(pl.multiple_of(t * 8, 8), 8), :] = v.reshape(24, 8, 128)
            return carry

        lax.fori_loop(0, 16, one, 0)

        def turn(t, carry):
            v = jnp.transpose(trans[t]).astype(BF16)
            outv[t, 128 * j:128 * (j + 1), :] = jnp.dot(v, select, preferred_element_type=F32).astype(BF16)
            return carry

        lax.fori_loop(0, 24, turn, 0)

    def put(j):
        cols = pl.ds(128 * j, 128)
        return pltpu.make_async_copy(outv.at[:, cols, :], out_ref.at[:, cols, :], loc_sem.at[j])

    for j in J:
        mixed(j)
        put(j).start()

    for j in range(3):
        give_coef(j).wait_send()
    give_ints.wait_send()
    swap.wait_send()
    for k in (1, 2, 3):
        fanx(k, 1).wait_send()
        fany(k, 1).wait_send()

    def drain(d, carry):
        for n in range(2):
            for j in range(2):
                ring(n, d, j, 1).wait_send()
            for w in range(4):
                fanz(n, d, w, 1).wait_send()
        return carry

    lax.fori_loop(1, 8, drain, 0)
    for n in range(2):
        ring(n, 8, n, 1).wait_send()
    for w in range(4):
        fanz(w // 2, 8, w, 1).wait_send()
    for n in range(2):
        for ch in range(2):
            mid(ch, n, 1).wait_send()
            midf(ch, n, 1).wait_send()
            for k in range(4):
                last(ch, k, n, 1).wait_send()
                lastf(ch, k, n, 1).wait_send()
        for j in range(3):
            hz(j, n, 1).wait_send()
            hzf(j, n, 1).wait_send()
            for k in range(4):
                hx(j, k, n, 1).wait_send()
                hxf(j, k, n, 1).wait_send()
    for j in range(3):
        for xk in range(4):
            for k in range(4):
                hp(j, xk, k, c).wait_send()
    for j in range(3):
        put(j).wait()


def on_device(integrals, coefficients, shell_starts, pair_ids):
    slot_count, batch_rows, ao_width = integrals.shape
    ints = integrals.reshape(slot_count * batch_rows, ao_width)
    D = pltpu.SemaphoreType.DMA
    pairs = [(3,), (1,), (2, 9, 2), (4,), (4,), (2, 9, 4), (2, 2), (2, 2), (2, 4, 2), (2, 4, 2),
             (1,), (3, 2), (3, 2), (3, 4, 2), (3, 4, 2), (3, 4, 4)]
    sems = [D((4,))]
    for shape in pairs:
        sems += [D(shape), D(shape)]
    out = pl.pallas_call(
        kernel,
        out_shape=jax.ShapeDtypeStruct((24, 384, 128), BF16),
        in_specs=[
            pl.BlockSpec(memory_space=pltpu.SMEM),
            pl.BlockSpec(memory_space=pltpu.VMEM),
            pl.BlockSpec(memory_space=pl.ANY),
            pl.BlockSpec(memory_space=pl.ANY),
        ],
        out_specs=pl.BlockSpec(memory_space=pl.ANY),
        scratch_shapes=[
            pltpu.VMEM((288, 8192), BF16),
            pltpu.VMEM((3, 4, 4, 4, 4, 32, 128), BF16),
            pltpu.VMEM((3, 2, 4, 4, 256, 128), BF16),
            pltpu.VMEM((2, 32, 384), BF16),
            pltpu.VMEM((192, 512), BF16),
            pltpu.VMEM((24, 128, 128), F32),
            pltpu.VMEM((24, 384, 128), BF16),
        ] + sems,
        compiler_params=pltpu.CompilerParams(
            collective_id=0, has_side_effects=True, vmem_limit_bytes=50 * 1024 * 1024),
    )(shell_starts, pair_ids, ints, coefficients)
    return out.reshape(2, 12, 384, 128)


def solution(mesh):
    return jax.shard_map(
        on_device,
        mesh=mesh,
        in_specs=(
            P(("coef", "pair"), None, None),
            P(None, ("coef", "pair"), None),
            P(),
            P("coef", None),
        ),
        out_specs=P(None, "pair", None, "coef"),
        check_vma=False,
    )
```

time: 1120 us -> 159 us (0.14)
  the two profiles are of different devices: /device:TPU:1 before, /device:TPU:32 now
where the time goes in v1:
time: 159 us
  Pallas kernels  152 us (96%)
  local copies, waits for them, and re-layouts  6.94 us (4%)
    pallas_call x1, Pallas kernels, on_device(): pl.pallas_call(kernel, out_shape=jax.ShapeDtypeStruct((24, 384, 128), BF1...  152 us
    unnamed x9, local copies, waits for them, and re-layouts  6.94 us

profile of v1, /device:TPU:32, one launch (start us, length us, event | category | flops | bytes accessed | tf_op | source)
XLA Modules:
  0.0 159.0 jit_solution(2200247839991526327)
XLA Ops:
  0.0 0.0 copy-start
  0.0 1.6 copy-done
  1.6 0.0 copy-start.1
  1.6 0.7 copy-done.1
  2.3 0.0 copy-start.2
  2.3 0.7 copy-done.2
  3.0 0.0 copy-start.3
  3.0 0.7 copy-done.3
  3.6 152.1 %shard_map.46 = bf16[24,384,128]{2,1,0:T(8,128)(2,1)} custom-call(s32[8]{0:T(128)S(1)} %copy-done.2, s32[1,128]{1,0:T(1,128)S(1)} %copy-done.3, bf16[128,8192]{1,0:T(8,128)(2,1)S(1)} %bitcast.2, bf16[2,16,384]{2,1,0:T(8,128)(2,1)S(1)} %copy-done.1), custom_call_target="tpu_custom_call" | custom-call | tf_op jit(solution)/shard_map/pallas_call | solution.py:443
  155.7 3.3 %copy.6 = bf16[2,12,384,128]{3,2,1,0:T(8,128)(2,1)} copy(bf16[2,12,384,128]{3,2,1,0:T(8,128)(2,1)} %bitcast.3) | data formatting | bytes 4718592
Async XLA Ops:
  0.0 1.6 %copy-start = (bf16[4,32,8192]{2,1,0:T(8,128)(2,1)S(1)}, bf16[4,32,8192]{2,1,0:T(8,128)(2,1)}, u32[]{:S(2)}) copy-start(bf16[4,32,8192]{2,1,0:T(8,128)(2,1)} %param.4) | copy-start | bytes 6291460
  1.6 0.7 copy-start.1
  2.3 0.7 copy-start.2
  3.0 0.7 copy-start.3

commit v2 on v1

v2 whole, which is shorter than its diff:
```python
import jax
import jax.numpy as jnp
from jax import lax
from jax.experimental import pallas as pl
from jax.experimental.pallas import tpu as pltpu
from jax.sharding import PartitionSpec as P

MESH = pl.DeviceIdType.MESH
SHW = 4
F32 = jnp.float32
BF16 = jnp.bfloat16


def kernel(starts_in, order_in, ints_ref, coef_ref, out_ref,
           starts_ref, order_ref, rows, panel, half, batch, mix, trans, outv, acc_ab, acc_c,
           loc_sem, cc_s, cc_r, ci_s, ci_r, ring_s, ring_r, fx_s, fx_r, fy_s, fy_r, fz_s, fz_r,
           mid_s, mid_r, midf_s, midf_r, last_s, last_r, lastf_s, lastf_r,
           b_s, b_r, hz_s, hz_r, hzf_s, hzf_r, hx_s, hx_r, hxf_s, hxf_r, hp_s, hp_r):
    a = lax.axis_index("coef")
    p = lax.axis_index("pair")
    zlo, y = a // 4, a % 4
    zhi, x, c = p // 8, (p // 2) % 4, p % 2
    z = zhi * 4 + zlo
    other = 1 - c

    def dev(z_, y_, x_, c_):
        return ((z_ % 4) * 4 + y_, (z_ // 4) * 8 + x_ * 2 + c_)

    def zz(k):
        return (z + k + 16) % 16

    def yy(k):
        return (y + k + 4) % 4

    def xx(k):
        return (x + k + 4) % 4

    def hh(k):
        return (zhi + k + 4) % 4

    partner = dev(z, y, x, other)
    z_to = (dev(zz(1), y, x, c), dev(zz(-1), y, x, c))
    z2_to = (dev(zz(2), y, x, c), dev(zz(-2), y, x, c))
    y_to = (dev(z, yy(1), x, c), dev(z, yy(-1), x, c))
    x_to = (dev(z, y, xx(1), c), dev(z, y, xx(-1), c))
    h_to = (dev(zz(4), y, x, c), dev(zz(-4), y, x, c))
    y_far = dev(z, yy(2), x, c)
    x_far = dev(z, y, xx(2), c)
    SIGN = (1, -1)

    def remote(ref, ssem, rsem, to):
        return pltpu.make_async_remote_copy(src_ref=ref, dst_ref=ref, send_sem=ssem, recv_sem=rsem,
                                            device_id=to, device_id_type=MESH)

    core_rows = pl.ds(pl.multiple_of(c * 16, 16), 16)
    int_rows = pl.ds(pl.multiple_of(c * 128, 128), 128)

    def own_coef(j):
        return pltpu.make_async_copy(coef_ref.at[c, :, pl.ds(128 * j, 128)],
                                     panel.at[j, 0, y, x, core_rows, :], loc_sem.at[j])

    own_ints = pltpu.make_async_copy(ints_ref, rows.at[int_rows, :], loc_sem.at[3])

    def give_coef(j):
        return pltpu.make_async_remote_copy(
            src_ref=coef_ref.at[other, :, pl.ds(128 * j, 128)],
            dst_ref=panel.at[j, 0, y, x, core_rows, :],
            send_sem=cc_s.at[j], recv_sem=cc_r.at[j], device_id=partner, device_id_type=MESH)

    def got_coef(j):
        ref = panel.at[j, 0, y, x, pl.ds(pl.multiple_of(other * 16, 16), 16), :]
        return remote(ref, cc_s.at[j], cc_r.at[j], partner)

    give_ints = pltpu.make_async_remote_copy(
        src_ref=ints_ref, dst_ref=rows.at[int_rows, :],
        send_sem=ci_s.at[0], recv_sem=ci_r.at[0], device_id=partner, device_id_type=MESH)
    got_ints = remote(rows.at[pl.ds(pl.multiple_of(other * 128, 128), 128), :], ci_s.at[0], ci_r.at[0], partner)

    for j in range(3):
        own_coef(j).start()
    own_ints.start()
    get_starts = pltpu.make_async_copy(starts_in, starts_ref, loc_sem.at[4])
    get_order = pltpu.make_async_copy(order_in, order_ref, loc_sem.at[5])
    get_starts.start()
    get_order.start()

    barrier = pltpu.get_barrier_semaphore()
    peers = (partner,) + z_to + z2_to + y_to + x_to + h_to + (y_far, x_far)
    for peer in peers:
        pl.semaphore_signal(barrier, inc=1, device_id=peer, device_id_type=MESH)
    pl.semaphore_wait(barrier, len(peers))

    for j in range(3):
        give_coef(j).start()
    give_ints.start()

    def slot(n, d):
        return 15 if d == 8 else (0 if d == 0 else 2 * d - 1 + n)

    def both(src, dst, ssem, rsem, to):
        return pltpu.make_async_remote_copy(src_ref=src, dst_ref=dst, send_sem=ssem, recv_sem=rsem,
                                            device_id=to, device_id_type=MESH)

    def ring(n, d):
        js = pl.ds(0, 2) if d < 8 else pl.ds(n, 1)
        src = panel.at[js, slot(n, max(d - 2, 0)), y, x]
        dst = panel.at[js, slot(n, d), y, x]
        return both(src, dst, ring_s.at[n, d], ring_r.at[n, d], (z_to if d == 1 else z2_to)[n])

    def fanx(k, back):
        to = (x_to[0], x_far, x_to[1])[k - 1]
        return remote(panel.at[2, 0, y, xx(-k * (1 - back))], fx_s.at[k], fx_r.at[k], to)

    def fany(k, back):
        to = (y_to[0], y_far, y_to[1])[k - 1]
        return remote(panel.at[2, 0, yy(-k * (1 - back))], fy_s.at[k], fy_r.at[k], to)

    def fanz(n, d, w):
        src = panel.at[2, slot(n, d - 1), w]
        dst = panel.at[2, slot(n, d), w]
        return both(src, dst, fz_s.at[n, d, w], fz_r.at[n, d, w], z_to[n])

    def ring_on(d):
        for n in range(2):
            ring(n, d).wait_recv()
            if d <= 6:
                ring(n, d + 2).start()

    def fanz_go(ws):
        for w in ws:
            for n in range(2):
                fanz(n, 1, w).start()

    def fanz_on(d, ws=(0, 1, 2, 3)):
        for w in ws:
            for n in range(2):
                if d < 8 or n == w // 2:
                    fanz(n, d, w).wait_recv()
                if d < 7 or (d == 7 and n == w // 2):
                    fanz(n, d + 1, w).start()

    own_coef(0).wait()
    got_coef(0).wait_recv()
    own_coef(1).wait()
    got_coef(1).wait_recv()
    for d in (1, 2):
        for n in range(2):
            ring(n, d).start()
    own_coef(2).wait()
    got_coef(2).wait_recv()
    for k in (1, 3, 2):
        fanx(k, 1).start()

    lane = lax.broadcasted_iota(jnp.int32, (32, 512), 1)
    row = lax.broadcasted_iota(jnp.int32, (32, 512), 0)
    get_starts.wait()
    get_order.wait()
    want = row % SHW
    for s in range(8):
        want = want + jnp.where(row // SHW == s, starts_ref[s], 0)

    def pick(q, carry):
        at = pl.multiple_of(q * 512, 512)
        rows[256:288, pl.ds(at, 512)] = jnp.where(lane + q * 512 == want, 1.0, 0.0).astype(BF16)
        return carry

    def spot(ch, m, l):
        return (l, m) if ch == 0 else (m, l)

    mid_to = (x_to, y_to)
    last_to = (y_to, x_to)
    here = (x, y)
    line = (y, x)

    def wrap(v, k):
        return (v + k + 4) % 4

    LOW = (0, 5, 9, 13)
    COUNT = (5, 4, 4, 3)

    def group(ch, g, y_, x_):
        return panel.at[ch, pl.ds(LOW[g], COUNT[g]), y_, x_]

    def group_half(ch, g, y_, x_, n):
        return panel.at[ch, pl.ds(LOW[g], COUNT[g]), y_, x_, pl.ds(16 * n, 16), :]

    def mid(ch, g, n, back):
        y_, x_ = spot(ch, wrap(here[ch], -SIGN[n] * (1 - back)), line[ch])
        return remote(group(ch, g, y_, x_), mid_s.at[ch, g, n], mid_r.at[ch, g, n], mid_to[ch][n])

    def midf(ch, g, n, back):
        y_, x_ = spot(ch, wrap(here[ch], -SIGN[n] * (2 - back)), line[ch])
        return remote(group_half(ch, g, y_, x_, n), midf_s.at[ch, g, n], midf_r.at[ch, g, n], mid_to[ch][n])

    def last(ch, g, k, n, back):
        y_, x_ = spot(ch, wrap(here[ch], k), wrap(line[ch], -SIGN[n] * (1 - back)))
        return remote(group(ch, g, y_, x_), last_s.at[ch, g, k, n], last_r.at[ch, g, k, n], last_to[ch][n])

    def lastf(ch, g, k, n, back):
        y_, x_ = spot(ch, wrap(here[ch], k), wrap(line[ch], -SIGN[n] * (2 - back)))
        return remote(group_half(ch, g, y_, x_, n), lastf_s.at[ch, g, k, n], lastf_r.at[ch, g, k, n],
                      last_to[ch][n])

    BOTH = [(ch, n) for ch in range(2) for n in range(2)]

    def p0(g):
        for ch, n in BOTH:
            mid(ch, g, n, 1).start()
        for ch, n in BOTH:
            last(ch, g, 0, n, 1).start()

    def p1(g):
        for ch, n in BOTH:
            mid(ch, g, n, 0).wait_recv()
            midf(ch, g, n, 1).start()
        for k in (1, 3):
            for ch, n in BOTH:
                last(ch, g, k, n, 1).start()

    def p2(g):
        for ch, n in BOTH:
            midf(ch, g, n, 0).wait_recv()
        for ch, n in BOTH:
            last(ch, g, 2, n, 1).start()

    def p3(g, *ks):
        for k in ks:
            for ch, n in BOTH:
                last(ch, g, k, n, 0).wait_recv()
                lastf(ch, g, k, n, 1).start()

    def columns(s):
        d = (s + 1) // 2
        o = (z + (1 - 2 * (s % 2)) * d + 32) % 16
        cuts = []
        for w in range(4):
            at = pl.multiple_of((((o % 4) * 4 + w) * 4 + o // 4) * 128, 128)
            cuts.append(rows[:, pl.ds(at, 128)])
        return jnp.concatenate(cuts, axis=1)

    def p4(g):
        for k in range(4):
            for ch, n in BOTH:
                lastf(ch, g, k, n, 0).wait_recv()

        def step(s, carry):
            block = jnp.concatenate([panel[0, s].reshape(512, 128), panel[1, s].reshape(512, 128)], axis=1)
            acc_ab[...] += jnp.dot(columns(s), block, preferred_element_type=F32)
            return carry

        lax.fori_loop(LOW[g], LOW[g] + COUNT[g], step, 0)

    def add_c(lo, hi):
        def step(s, carry):
            acc_c[...] += jnp.dot(columns(s), panel[2, s].reshape(512, 128), preferred_element_type=F32)
            return carry

        lax.fori_loop(lo, hi, step, 0)

    ring_on(1)
    for k in (1, 3, 2):
        fanx(k, 0).wait_recv()
    for k in (1, 3, 2):
        fany(k, 1).start()
    ring_on(2)
    p0(0)
    lax.fori_loop(0, 16, pick, 0)
    acc_ab[...] = jnp.zeros_like(acc_ab)
    acc_c[...] = jnp.zeros_like(acc_c)
    ring_on(3)
    ring_on(4)
    p0(1)
    for k in (1, 3, 2):
        fany(k, 0).wait_recv()
    fanz_go((0, 1))
    p1(0)
    ring_on(5)
    ring_on(6)
    p0(2)
    fanz_go((2, 3))
    p2(0)
    p1(1)
    fanz_on(1, (0, 1))
    ring_on(7)
    for n in range(2):
        ring(n, 8).wait_recv()
    p0(3)
    p3(0, 0)
    fanz_on(1, (2, 3))
    p2(1)
    p1(2)
    p3(1, 0)
    p3(0, 1, 3)
    fanz_on(2)
    p1(3)
    p2(2)
    p3(0, 2)
    p3(2, 0)
    p3(1, 1, 3)
    fanz_on(3)
    p2(3)
    p3(1, 2)
    p3(3, 0)
    p3(2, 1, 3)
    own_ints.wait()
    got_ints.wait_recv()
    fanz_on(4)
    p3(2, 2)
    p3(3, 1, 3)
    p4(0)
    fanz_on(5)
    p3(3, 2)
    p4(1)
    add_c(0, 7)
    fanz_on(6)
    p4(2)
    fanz_on(7)
    add_c(7, 13)

    def piece(j, c_, x_, h_):
        return half.at[j, c_, x_, h_]

    def part(j, c_, x_, h_, n):
        return half.at[j, c_, x_, h_, pl.ds(128 * n, 128), :]

    def hz(j, n, back):
        return remote(piece(j, c, x, hh(-SIGN[n] * (1 - back))), hz_s.at[j, n], hz_r.at[j, n], h_to[n])

    def hzf(j, n, back):
        return remote(part(j, c, x, hh(-SIGN[n] * (2 - back)), n), hzf_s.at[j, n], hzf_r.at[j, n], h_to[n])

    def hx(j, k, n, back):
        return remote(piece(j, c, xx(-SIGN[n] * (1 - back)), hh(k)), hx_s.at[j, k, n], hx_r.at[j, k, n], x_to[n])

    def hxf(j, k, n, back):
        return remote(part(j, c, xx(-SIGN[n] * (2 - back)), hh(k), n), hxf_s.at[j, k, n], hxf_r.at[j, k, n], x_to[n])

    def hp(j, xk, k, c_):
        return remote(piece(j, c_, xx(xk), hh(k)), hp_s.at[j, xk, k], hp_r.at[j, xk, k], partner)

    def save(j, v):
        half[j, c, x, zhi] = v[:256].astype(BF16)
        batch[c, :, 128 * j:128 * (j + 1)] = v[256:].astype(BF16)

    def spread(j, k):
        for n in range(2):
            hx(j, k, n, 1).start()
        hp(j, 0, k, c).start()

    def e0(j):
        for n in range(2):
            hz(j, n, 1).start()
        spread(j, 0)

    def e1(j):
        for n in range(2):
            hz(j, n, 0).wait_recv()
            hzf(j, n, 1).start()
        spread(j, 1)
        spread(j, 3)

    def e2(j):
        for n in range(2):
            hzf(j, n, 0).wait_recv()
        spread(j, 2)

    def x1(j, k):
        for n in range(2):
            hx(j, k, n, 0).wait_recv()
            hxf(j, k, n, 1).start()
        hp(j, 3, k, c).start()
        hp(j, 1, k, c).start()

    def x2(j, k):
        for n in range(2):
            hxf(j, k, n, 0).wait_recv()
        hp(j, 2, k, c).start()

    p4(3)
    save(0, acc_ab[:, 0:128])
    e0(0)
    save(1, acc_ab[:, 128:256])
    e0(1)
    fanz_on(8)
    add_c(13, 16)
    save(2, acc_c[...])
    swap = remote(batch.at[c], b_s.at[0], b_r.at[0], partner)
    swap.start()
    x1(0, 0)
    x1(1, 0)
    e1(0)
    e0(2)
    x2(0, 0)
    x2(1, 0)
    remote(batch.at[other], b_s.at[0], b_r.at[0], partner).wait_recv()

    r96 = lax.broadcasted_iota(jnp.int32, (96, 384), 0)
    c384 = lax.broadcasted_iota(jnp.int32, (96, 384), 1)
    chosen = jnp.where(c384 == p * 12 + r96 // 8, 1.0, 0.0).astype(BF16)
    r256 = lax.broadcasted_iota(jnp.int32, (96, 256), 0)
    c256 = lax.broadcasted_iota(jnp.int32, (96, 256), 1)
    same = r256 % 8 == c256 // 32
    grid = []
    for t in range(2):
        wide = jnp.concatenate([batch[t]] * 8, axis=0)
        g = lax.dot_general(chosen, wide, (((1,), (1,)), ((), ())), preferred_element_type=F32)
        grid.append(jnp.where(same, g, 0.0))
    mix[0:96, 0:256] = grid[0].astype(BF16)
    mix[0:96, 256:512] = grid[1].astype(BF16)
    mix[96:192, 0:256] = (-grid[1]).astype(BF16)
    mix[96:192, 256:512] = grid[0].astype(BF16)
    spots = lax.broadcasted_iota(jnp.int32, (128, 128), 0)
    select = jnp.transpose(jnp.where(spots == order_ref[0:1, :], 1.0, 0.0)).astype(BF16)

    def hp_wait(j, ks):
        for xk in range(4):
            for k in ks:
                hp(j, xk, k, other).wait_recv()

    def mixed(js, ks):
        lo, n = js[0], len(js)

        def one(t, carry):
            for k in ks:
                h_, x_ = hh(k), t
                v = jnp.zeros((192, 128 * n), F32)
                for t_ in range(2):
                    b = jnp.concatenate([half[j, t_, x_, h_] for j in js], axis=1)
                    v = v + jnp.dot(mix[:, 256 * t_:256 * (t_ + 1)], b, preferred_element_type=F32)
                at = pl.ds(pl.multiple_of((h_ * 4 + x_) * 8, 8), 8)
                for i, j in enumerate(js):
                    trans[j, :, at, :] = v[:, 128 * i:128 * (i + 1)].reshape(24, 8, 128)
            return carry

        lax.fori_loop(0, 4, one, 0)

    def turn(j):
        def some(t, carry):
            for u in range(4):
                v = jnp.transpose(trans[j, t * 4 + u]).astype(BF16)
                outv[t * 4 + u, 128 * j:128 * (j + 1), :] = jnp.dot(
                    v, select, preferred_element_type=F32).astype(BF16)
            return carry

        lax.fori_loop(0, 6, some, 0)

    e1(1)
    x1(2, 0)
    x1(0, 1)
    x1(0, 3)
    x1(1, 1)
    x1(1, 3)
    x2(0, 1)
    x2(0, 3)
    e1(2)
    hp_wait(0, (0,))
    hp_wait(1, (0,))
    mixed((0, 1), (0,))
    x2(1, 1)
    x2(1, 3)
    x2(2, 0)
    e2(0)
    x1(2, 1)
    x1(2, 3)
    e2(1)
    hp_wait(0, (1, 3))
    hp_wait(1, (1, 3))
    mixed((0, 1), (1, 3))
    x1(0, 2)
    x2(2, 1)
    x2(2, 3)
    x1(1, 2)
    e2(2)
    hp_wait(2, (0,))
    mixed((2,), (0,))
    x2(0, 2)
    x2(1, 2)
    x1(2, 2)
    hp_wait(0, (2,))
    hp_wait(1, (2,))
    mixed((0, 1), (2,))
    x2(2, 2)
    turn(0)
    def put(j):
        cols = pl.ds(128 * j, 128)
        return pltpu.make_async_copy(outv.at[:, cols, :], out_ref.at[:, cols, :], loc_sem.at[j])

    put(0).start()
    hp_wait(2, (1, 3))
    mixed((2,), (1, 3))
    turn(1)
    put(1).start()
    hp_wait(2, (2,))
    mixed((2,), (2,))
    turn(2)
    put(2).start()

    for j in range(3):
        give_coef(j).wait_send()
    give_ints.wait_send()
    swap.wait_send()
    for k in (1, 2, 3):
        fanx(k, 1).wait_send()
        fany(k, 1).wait_send()

    for n in range(2):
        for d in range(1, 9):
            ring(n, d).wait_send()
            for w in range(4):
                if d < 8 or n == w // 2:
                    fanz(n, d, w).wait_send()
    for n in range(2):
        for ch in range(2):
            for g in range(4):
                mid(ch, g, n, 1).wait_send()
                midf(ch, g, n, 1).wait_send()
                for k in range(4):
                    last(ch, g, k, n, 1).wait_send()
                    lastf(ch, g, k, n, 1).wait_send()
        for j in range(3):
            hz(j, n, 1).wait_send()
            hzf(j, n, 1).wait_send()
            for k in range(4):
                hx(j, k, n, 1).wait_send()
                hxf(j, k, n, 1).wait_send()
    for j in range(3):
        for xk in range(4):
            for k in range(4):
                hp(j, xk, k, c).wait_send()
    for j in range(3):
        put(j).wait()


def on_device(integrals, coefficients, shell_starts, pair_ids):
    slot_count, batch_rows, ao_width = integrals.shape
    ints = integrals.reshape(slot_count * batch_rows, ao_width)
    D = pltpu.SemaphoreType.DMA
    pairs = [(3,), (1,), (2, 9), (4,), (4,), (2, 9, 4), (2, 4, 2), (2, 4, 2), (2, 4, 4, 2), (2, 4, 4, 2),
             (1,), (3, 2), (3, 2), (3, 4, 2), (3, 4, 2), (3, 4, 4)]
    sems = [D((6,))]
    for shape in pairs:
        sems += [D(shape), D(shape)]
    out = pl.pallas_call(
        kernel,
        out_shape=jax.ShapeDtypeStruct((24, 384, 128), BF16),
        in_specs=[
            pl.BlockSpec(memory_space=pltpu.HBM),
            pl.BlockSpec(memory_space=pltpu.HBM),
            pl.BlockSpec(memory_space=pltpu.HBM),
            pl.BlockSpec(memory_space=pltpu.HBM),
        ],
        out_specs=pl.BlockSpec(memory_space=pl.ANY),
        scratch_shapes=[
            pltpu.SMEM((8,), jnp.int32),
            pltpu.VMEM((1, 128), jnp.int32),
            pltpu.VMEM((288, 8192), BF16),
            pltpu.VMEM((3, 16, 4, 4, 32, 128), BF16),
            pltpu.VMEM((3, 2, 4, 4, 256, 128), BF16),
            pltpu.VMEM((2, 32, 384), BF16),
            pltpu.VMEM((192, 512), BF16),
            pltpu.VMEM((3, 24, 128, 128), F32),
            pltpu.VMEM((24, 384, 128), BF16),
            pltpu.VMEM((288, 256), F32),
            pltpu.VMEM((288, 128), F32),
        ] + sems,
        compiler_params=pltpu.CompilerParams(
            collective_id=0, has_side_effects=True, vmem_limit_bytes=67043328),
    )(shell_starts, pair_ids, ints, coefficients)
    return out.reshape(2, 12, 384, 128)


def solution(mesh):
    return jax.shard_map(
        on_device,
        mesh=mesh,
        in_specs=(
            P(("coef", "pair"), None, None),
            P(None, ("coef", "pair"), None),
            P(),
            P("coef", None),
        ),
        out_specs=P(None, "pair", None, "coef"),
        check_vma=False,
    )
```

time: 159 us -> 118 us (0.74)
  the two profiles are of different devices: /device:TPU:32 before, /device:TPU:1 now
where the time goes in v2:
time: 118 us; the launch traced here: 116 us
  Pallas kernels  113 us (96%)
  local copies, waits for them, and re-layouts  3.3 us (3%)
    pallas_call x1, Pallas kernels, on_device(): pl.pallas_call(kernel, out_shape=jax.ShapeDtypeStruct((24, 384, 128), BF1...  113 us
    unnamed x1, local copies, waits for them, and re-layouts  3.3 us

profile of v2, /device:TPU:1, one launch (start us, length us, event | category | flops | bytes accessed | tf_op | source)
XLA Modules:
  0.0 116.1 jit_solution(3132536683710430839)
XLA Ops:
  0.0 112.8 %shard_map.46 = bf16[24,384,128]{2,1,0:T(8,128)(2,1)} custom-call(s32[8]{0:T(128)} %starts_in.1, s32[1,128]{1,0:T(1,128)} %order_in.1, bf16[128,8192]{1,0:T(8,128)(2,1)} %bitcast.3, bf16[2,16,384]{2,1,0:T(8,128)(2,1)} %coef_ref.1), custom_call_target="tpu_custom_call" | custom-call | tf_op jit(solution)/shard_map/pallas_call | solution.py:543
  112.8 3.3 %copy.6 = bf16[2,12,384,128]{3,2,1,0:T(8,128)(2,1)} copy(bf16[2,12,384,128]{3,2,1,0:T(8,128)(2,1)} %bitcast.2) | data formatting | bytes 4718592

commit v3 on v2

v3 whole, which is shorter than its diff:
```python
import jax
import jax.numpy as jnp
from jax import lax
from jax.experimental import pallas as pl
from jax.experimental.pallas import tpu as pltpu
from jax.sharding import PartitionSpec as P

MESH = pl.DeviceIdType.MESH
SHW = 4
F32 = jnp.float32
BF16 = jnp.bfloat16


def kernel(starts_in, order_in, ints_ref, coef_ref, out_ref,
           starts_ref, order_ref, rows, panel, half, batch, mix, trans, outv, acc,
           loc_sem, cc_s, cc_r, ci_s, ci_r, ring_s, ring_r,
           mid_s, mid_r, midf_s, midf_r, last_s, last_r, lastf_s, lastf_r,
           b_s, b_r, hz_s, hz_r, hzf_s, hzf_r, hx_s, hx_r, hxf_s, hxf_r, hp_s, hp_r):
    a = lax.axis_index("coef")
    p = lax.axis_index("pair")
    zlo, y = a // 4, a % 4
    zhi, x, c = p // 8, (p // 2) % 4, p % 2
    z = zhi * 4 + zlo
    other = 1 - c

    def dev(z_, y_, x_, c_):
        return ((z_ % 4) * 4 + y_, (z_ // 4) * 8 + x_ * 2 + c_)

    def zz(k):
        return (z + k + 16) % 16

    def yy(k):
        return (y + k + 4) % 4

    def xx(k):
        return (x + k + 4) % 4

    def hh(k):
        return (zhi + k + 4) % 4

    partner = dev(z, y, x, other)
    z_to = (dev(zz(1), y, x, c), dev(zz(-1), y, x, c))
    z2_to = (dev(zz(2), y, x, c), dev(zz(-2), y, x, c))
    y_to = (dev(z, yy(1), x, c), dev(z, yy(-1), x, c))
    x_to = (dev(z, y, xx(1), c), dev(z, y, xx(-1), c))
    h_to = (dev(zz(4), y, x, c), dev(zz(-4), y, x, c))
    SIGN = (1, -1)

    def remote(ref, ssem, rsem, to):
        return pltpu.make_async_remote_copy(src_ref=ref, dst_ref=ref, send_sem=ssem, recv_sem=rsem,
                                            device_id=to, device_id_type=MESH)

    core_rows = pl.ds(pl.multiple_of(c * 16, 16), 16)
    int_rows = pl.ds(pl.multiple_of(c * 128, 128), 128)

    def own_coef(j):
        return pltpu.make_async_copy(coef_ref.at[c, :, pl.ds(128 * j, 128)],
                                     panel.at[j, 0, y, x, core_rows, :], loc_sem.at[j])

    own_ints = pltpu.make_async_copy(ints_ref, rows.at[int_rows, :], loc_sem.at[3])

    def give_coef(j):
        return pltpu.make_async_remote_copy(
            src_ref=coef_ref.at[other, :, pl.ds(128 * j, 128)],
            dst_ref=panel.at[j, 0, y, x, core_rows, :],
            send_sem=cc_s.at[j], recv_sem=cc_r.at[j], device_id=partner, device_id_type=MESH)

    def got_coef(j):
        ref = panel.at[j, 0, y, x, pl.ds(pl.multiple_of(other * 16, 16), 16), :]
        return remote(ref, cc_s.at[j], cc_r.at[j], partner)

    give_ints = pltpu.make_async_remote_copy(
        src_ref=ints_ref, dst_ref=rows.at[int_rows, :],
        send_sem=ci_s.at[0], recv_sem=ci_r.at[0], device_id=partner, device_id_type=MESH)
    got_ints = remote(rows.at[pl.ds(pl.multiple_of(other * 128, 128), 128), :], ci_s.at[0], ci_r.at[0], partner)

    for j in range(3):
        own_coef(j).start()
    own_ints.start()
    get_starts = pltpu.make_async_copy(starts_in, starts_ref, loc_sem.at[4])
    get_order = pltpu.make_async_copy(order_in, order_ref, loc_sem.at[5])
    get_starts.start()
    get_order.start()

    barrier = pltpu.get_barrier_semaphore()
    peers = (partner,) + z_to + z2_to + y_to + x_to + h_to
    for peer in peers:
        pl.semaphore_signal(barrier, inc=1, device_id=peer, device_id_type=MESH)
    pl.semaphore_wait(barrier, len(peers))

    for j in range(3):
        give_coef(j).start()
    give_ints.start()

    def slot(n, d):
        return 15 if d == 8 else (0 if d == 0 else 2 * d - 1 + n)

    def both(src, dst, ssem, rsem, to):
        return pltpu.make_async_remote_copy(src_ref=src, dst_ref=dst, send_sem=ssem, recv_sem=rsem,
                                            device_id=to, device_id_type=MESH)

    def ring(n, d):
        row_part = pl.ds(0, 32) if d < 8 else pl.ds(16 * n, 16)
        src = panel.at[:, slot(n, max(d - 2, 0)), y, x, row_part, :]
        dst = panel.at[:, slot(n, d), y, x, row_part, :]
        return both(src, dst, ring_s.at[n, d], ring_r.at[n, d], (z_to if d == 1 else z2_to)[n])

    def ring_on(d):
        for n in range(2):
            ring(n, d).wait_recv()
            if d <= 6:
                ring(n, d + 2).start()

    for j in range(3):
        own_coef(j).wait()
        got_coef(j).wait_recv()
    for d in (1, 2):
        for n in range(2):
            ring(n, d).start()

    lane = lax.broadcasted_iota(jnp.int32, (32, 512), 1)
    row = lax.broadcasted_iota(jnp.int32, (32, 512), 0)
    get_starts.wait()
    get_order.wait()
    want = row % SHW
    for s in range(8):
        want = want + jnp.where(row // SHW == s, starts_ref[s], 0)

    def pick(q, carry):
        at = pl.multiple_of(q * 512, 512)
        rows[256:288, pl.ds(at, 512)] = jnp.where(lane + q * 512 == want, 1.0, 0.0).astype(BF16)
        return carry

    def spot(ch, m, l):
        return (l, m) if ch == 0 else (m, l)

    mid_to = (x_to, y_to)
    last_to = (y_to, x_to)
    here = (x, y)
    line = (y, x)

    def wrap(v, k):
        return (v + k + 4) % 4

    UNIT = (
        (0, 5, (0, 1), (0, 1), True),
        (5, 4, (0, 1), (0, 1), True),
        (9, 4, (0, 1), (0, 1), True),
        (13, 3, (0, 1), (0, 1), True),
        (0, 8, (0, 1), (2, 2), False),
        (8, 8, (0, 1), (2, 2), False),
    )

    def span(ch, g, y_, x_, lo, count):
        _, _, routes, chunks, whole = UNIT[g]
        j = chunks[routes.index(ch)]
        if whole:
            return panel.at[j, pl.ds(lo, count), y_, x_]
        return panel.at[j, pl.ds(lo, count), y_, x_, pl.ds(16 * ch, 16), :]

    def group(ch, g, y_, x_):
        return span(ch, g, y_, x_, UNIT[g][0], UNIT[g][1])

    def group_half(ch, g, y_, x_, n):
        lo, count, routes, chunks, whole = UNIT[g]
        if whole:
            return panel.at[chunks[routes.index(ch)], pl.ds(lo, count), y_, x_, pl.ds(16 * n, 16), :]
        first = (count + 1) // 2
        return span(ch, g, y_, x_, lo + n * first, count - first if n else first)

    def mid(ch, g, n, back):
        y_, x_ = spot(ch, wrap(here[ch], -SIGN[n] * (1 - back)), line[ch])
        return remote(group(ch, g, y_, x_), mid_s.at[ch, g, n], mid_r.at[ch, g, n], mid_to[ch][n])

    def midf(ch, g, n, back):
        y_, x_ = spot(ch, wrap(here[ch], -SIGN[n] * (2 - back)), line[ch])
        return remote(group_half(ch, g, y_, x_, n), midf_s.at[ch, g, n], midf_r.at[ch, g, n], mid_to[ch][n])

    def last(ch, g, k, n, back):
        y_, x_ = spot(ch, wrap(here[ch], k), wrap(line[ch], -SIGN[n] * (1 - back)))
        return remote(group(ch, g, y_, x_), last_s.at[ch, g, k, n], last_r.at[ch, g, k, n], last_to[ch][n])

    def lastf(ch, g, k, n, back):
        y_, x_ = spot(ch, wrap(here[ch], k), wrap(line[ch], -SIGN[n] * (2 - back)))
        return remote(group_half(ch, g, y_, x_, n), lastf_s.at[ch, g, k, n], lastf_r.at[ch, g, k, n],
                      last_to[ch][n])

    def both_of(g):
        return [(ch, n) for ch in UNIT[g][2] for n in range(2)]

    def m0(*gs):
        for g in gs:
            for ch, n in both_of(g):
                mid(ch, g, n, 1).start()

    def l0(g):
        for ch, n in both_of(g):
            last(ch, g, 0, n, 1).start()

    def p1m(*gs):
        for g in gs:
            for ch, n in both_of(g):
                mid(ch, g, n, 0).wait_recv()
                midf(ch, g, n, 1).start()

    def p1l(g):
        for k in (1, 3):
            for ch, n in both_of(g):
                last(ch, g, k, n, 1).start()

    def p2(g):
        for ch, n in both_of(g):
            midf(ch, g, n, 0).wait_recv()
        for ch, n in both_of(g):
            last(ch, g, 2, n, 1).start()

    def p3(g, *ks):
        for k in ks:
            for ch, n in both_of(g):
                last(ch, g, k, n, 0).wait_recv()
                lastf(ch, g, k, n, 1).start()

    def columns(s):
        d = (s + 1) // 2
        o = (z + (1 - 2 * (s % 2)) * d + 32) % 16
        cuts = []
        for w in range(4):
            at = pl.multiple_of((((o % 4) * 4 + w) * 4 + o // 4) * 128, 128)
            cuts.append(rows[:, pl.ds(at, 128)])
        return jnp.concatenate(cuts, axis=1)

    def p4(g):
        for k in range(4):
            for ch, n in both_of(g):
                lastf(ch, g, k, n, 0).wait_recv()

        lo, count, _, chunks, _ = UNIT[g]
        js = tuple(sorted(set(chunks)))

        def step(s, carry):
            block = jnp.concatenate([panel[j, s].reshape(512, 128) for j in js], axis=1)
            v = jnp.dot(columns(s), block, preferred_element_type=F32)
            for i, j in enumerate(js):
                acc[j] += v[:, 128 * i:128 * (i + 1)]
            return carry

        lax.fori_loop(lo, lo + count, step, 0, unroll=2)

    def piece(j, c_, x_, h_):
        return half.at[j, c_, x_, h_]

    def part(j, c_, x_, h_, n):
        return half.at[j, c_, x_, h_, pl.ds(128 * n, 128), :]

    def hz(j, n, h, back):
        return remote(part(j, c, x, hh(-SIGN[n] * (1 - back)), h), hz_s.at[j, n, h], hz_r.at[j, n, h], h_to[n])

    def hzf(j, n, back):
        return remote(part(j, c, x, hh(-SIGN[n] * (2 - back)), n), hzf_s.at[j, n], hzf_r.at[j, n], h_to[n])

    def hx(j, k, n, back):
        return remote(piece(j, c, xx(-SIGN[n] * (1 - back)), hh(k)), hx_s.at[j, k, n], hx_r.at[j, k, n], x_to[n])

    def hxf(j, k, n, back):
        return remote(part(j, c, xx(-SIGN[n] * (2 - back)), hh(k), n), hxf_s.at[j, k, n], hxf_r.at[j, k, n], x_to[n])

    def hp(j, xk, k, c_):
        return remote(piece(j, c_, xx(xk), hh(k)), hp_s.at[j, xk, k], hp_r.at[j, xk, k], partner)

    def save(j):
        v = acc[j]
        half[j, c, x, zhi] = v[:256].astype(BF16)
        batch[c, :, 128 * j:128 * (j + 1)] = v[256:].astype(BF16)

    def spread(j, k):
        for n in range(2):
            hx(j, k, n, 1).start()
        hp(j, 0, k, c).start()

    def e0(j):
        for n in range(2):
            hz(j, n, n, 1).start()
        for n in range(2):
            hz(j, n, 1 - n, 1).start()
        spread(j, 0)

    def e1a(j):
        for n in range(2):
            hz(j, n, n, 0).wait_recv()
            hzf(j, n, 1).start()

    def e1b(j):
        for n in range(2):
            hz(j, n, 1 - n, 0).wait_recv()
        spread(j, 1)
        spread(j, 3)

    def e2(j):
        for n in range(2):
            hzf(j, n, 0).wait_recv()
        spread(j, 2)

    def x1(j, k):
        for n in range(2):
            hx(j, k, n, 0).wait_recv()
            hxf(j, k, n, 1).start()
        hp(j, 3, k, c).start()
        hp(j, 1, k, c).start()

    def x2(j, k):
        for n in range(2):
            hxf(j, k, n, 0).wait_recv()
        hp(j, 2, k, c).start()

    swap = remote(batch.at[c], b_s.at[0], b_r.at[0], partner)

    def blend():
        remote(batch.at[other], b_s.at[0], b_r.at[0], partner).wait_recv()
        r96 = lax.broadcasted_iota(jnp.int32, (96, 384), 0)
        c384 = lax.broadcasted_iota(jnp.int32, (96, 384), 1)
        chosen = jnp.where(c384 == p * 12 + r96 // 8, 1.0, 0.0).astype(BF16)
        r256 = lax.broadcasted_iota(jnp.int32, (96, 256), 0)
        c256 = lax.broadcasted_iota(jnp.int32, (96, 256), 1)
        same = r256 % 8 == c256 // 32
        grid = []
        for t in range(2):
            wide = jnp.concatenate([batch[t]] * 8, axis=0)
            g = lax.dot_general(chosen, wide, (((1,), (1,)), ((), ())), preferred_element_type=F32)
            grid.append(jnp.where(same, g, 0.0))
        mix[0:96, 0:256] = grid[0].astype(BF16)
        mix[0:96, 256:512] = grid[1].astype(BF16)
        mix[96:192, 0:256] = (-grid[1]).astype(BF16)
        mix[96:192, 256:512] = grid[0].astype(BF16)
        spots = lax.broadcasted_iota(jnp.int32, (128, 128), 0)
        select = jnp.transpose(jnp.where(spots == order_ref[0:1, :], 1.0, 0.0)).astype(BF16)
        return select

    def hp_wait(j, ks):
        for xk in range(4):
            for k in ks:
                hp(j, xk, k, other).wait_recv()

    def mixed(js, ks):
        n = len(js)

        for k in ks:
            h_ = hh(k)
            for x_ in range(4):
                v = jnp.zeros((192, 128 * n), F32)
                for t_ in range(2):
                    b = jnp.concatenate([half[j, t_, x_, h_] for j in js], axis=1)
                    v = v + jnp.dot(mix[:, 256 * t_:256 * (t_ + 1)], b, preferred_element_type=F32)
                at = pl.ds(pl.multiple_of((h_ * 4 + x_) * 8, 8), 8)
                for i, j in enumerate(js):
                    trans[j, :, at, :] = v[:, 128 * i:128 * (i + 1)].reshape(24, 8, 128)

    def turn(j, select):
        def some(t, carry):
            for u in range(4):
                v = jnp.transpose(trans[j, t * 4 + u]).astype(BF16)
                outv[t * 4 + u, 128 * j:128 * (j + 1), :] = jnp.dot(
                    v, select, preferred_element_type=F32).astype(BF16)
            return carry

        lax.fori_loop(0, 6, some, 0)

    def put(j):
        cols = pl.ds(128 * j, 128)
        return pltpu.make_async_copy(outv.at[:, cols, :], out_ref.at[:, cols, :], loc_sem.at[j])

    lax.fori_loop(0, 16, pick, 0)
    acc[...] = jnp.zeros_like(acc)
    ring_on(1)
    ring_on(2)
    m0(0)
    l0(0)
    ring_on(3)
    p1m(0)
    p1l(0)
    ring_on(4)
    l0(1)
    m0(1)
    p2(0)
    p3(0, 1)
    p3(0, 0)
    ring_on(5)
    ring_on(6)
    l0(2)
    m0(2)
    p1m(1)
    m0(4)
    p1l(1)
    ring_on(7)
    ring_on(8)
    m0(3)
    l0(3)
    p1m(2)
    p1l(2)
    p3(0, 2)
    p3(1, 0)
    p3(0, 3)
    p1m(3)
    p2(1)
    p2(2)
    p3(2, 0)
    p1l(3)
    p3(2, 1)
    p2(3)
    p3(1, 1)
    p3(2, 3)
    p3(1, 2)
    p3(2, 2)
    p3(1, 3)
    m0(5)
    p3(3, 0)
    p3(3, 3)
    own_ints.wait()
    got_ints.wait_recv()
    p4(0)
    p3(3, 2)
    p3(3, 1)
    p1m(4)
    p1l(4)
    l0(4)
    p4(2)
    p1m(5)
    p1l(5)
    p4(1)
    l0(5)
    p4(3)
    save(0)
    e0(0)
    p2(5)
    save(1)
    e0(1)
    p3(5, 1)
    p2(4)
    p3(5, 0)
    p3(5, 3)
    p3(5, 2)
    x1(0, 0)
    p3(4, 1)
    p3(4, 0)
    p3(4, 3)
    p3(4, 2)
    x1(1, 0)
    x2(0, 0)
    e1a(0)
    e1b(0)
    p4(5)
    p4(4)
    save(2)
    e0(2)
    x1(0, 1)
    e1a(1)
    e1b(1)
    e2(0)
    x1(1, 1)
    x1(0, 3)
    swap.start()
    x1(1, 3)
    e1a(2)
    x1(0, 2)
    select = blend()
    x1(2, 0)
    e1b(2)
    x2(0, 2)
    e2(1)
    hp_wait(0, (2,))
    mixed((0,), (2,))
    x2(1, 3)
    hp_wait(0, (0,))
    mixed((0,), (0,))
    x2(1, 0)
    x2(1, 1)
    x1(2, 1)
    x2(2, 0)
    e2(2)
    x2(0, 3)
    x2(0, 1)
    x1(2, 3)
    x1(1, 2)
    hp_wait(1, (3,))
    mixed((1,), (3,))
    hp_wait(0, (3,))
    mixed((0,), (3,))
    hp_wait(0, (1,))
    mixed((0,), (1,))
    turn(0, select)
    put(0).start()
    x1(2, 2)
    hp_wait(2, (0,))
    mixed((2,), (0,))
    x2(2, 1)
    hp_wait(1, (0,))
    mixed((1,), (0,))
    x2(2, 3)
    hp_wait(1, (1,))
    mixed((1,), (1,))
    x2(1, 2)
    hp_wait(2, (1,))
    mixed((2,), (1,))
    hp_wait(2, (3,))
    mixed((2,), (3,))
    hp_wait(1, (2,))
    mixed((1,), (2,))
    x2(2, 2)
    turn(1, select)
    put(1).start()
    hp_wait(2, (2,))
    mixed((2,), (2,))
    turn(2, select)
    put(2).start()

    for j in range(3):
        give_coef(j).wait_send()
    give_ints.wait_send()
    swap.wait_send()

    for n in range(2):
        for d in range(1, 9):
            ring(n, d).wait_send()
    for n in range(2):
        for g in range(6):
            for ch in UNIT[g][2]:
                mid(ch, g, n, 1).wait_send()
                midf(ch, g, n, 1).wait_send()
                for k in range(4):
                    last(ch, g, k, n, 1).wait_send()
                    lastf(ch, g, k, n, 1).wait_send()
        for j in range(3):
            hz(j, n, 0, 1).wait_send()
            hz(j, n, 1, 1).wait_send()
            hzf(j, n, 1).wait_send()
            for k in range(4):
                hx(j, k, n, 1).wait_send()
                hxf(j, k, n, 1).wait_send()
    for j in range(3):
        for xk in range(4):
            for k in range(4):
                hp(j, xk, k, c).wait_send()
    for j in range(3):
        put(j).wait()


def on_device(integrals, coefficients, shell_starts, pair_ids):
    slot_count, batch_rows, ao_width = integrals.shape
    ints = integrals.reshape(slot_count * batch_rows, ao_width)
    D = pltpu.SemaphoreType.DMA
    pairs = [(3,), (1,), (2, 9), (2, 6, 2), (2, 6, 2), (2, 6, 4, 2), (2, 6, 4, 2),
             (1,), (3, 2, 2), (3, 2), (3, 4, 2), (3, 4, 2), (3, 4, 4)]
    sems = [D((6,))]
    for shape in pairs:
        sems += [D(shape), D(shape)]
    out = pl.pallas_call(
        kernel,
        out_shape=jax.ShapeDtypeStruct((24, 384, 128), BF16),
        in_specs=[
            pl.BlockSpec(memory_space=pltpu.HBM),
            pl.BlockSpec(memory_space=pltpu.HBM),
            pl.BlockSpec(memory_space=pltpu.HBM),
            pl.BlockSpec(memory_space=pltpu.HBM),
        ],
        out_specs=pl.BlockSpec(memory_space=pl.ANY),
        scratch_shapes=[
            pltpu.SMEM((8,), jnp.int32),
            pltpu.VMEM((1, 128), jnp.int32),
            pltpu.VMEM((288, 8192), BF16),
            pltpu.VMEM((3, 16, 4, 4, 32, 128), BF16),
            pltpu.VMEM((3, 2, 4, 4, 256, 128), BF16),
            pltpu.VMEM((2, 32, 384), BF16),
            pltpu.VMEM((192, 512), BF16),
            pltpu.VMEM((3, 24, 128, 128), F32),
            pltpu.VMEM((24, 384, 128), BF16),
            pltpu.VMEM((3, 288, 128), F32),
        ] + sems,
        compiler_params=pltpu.CompilerParams(
            collective_id=0, has_side_effects=True, vmem_limit_bytes=40000000),
    )(*[pltpu.with_memory_space_constraint(v, pltpu.HBM) for v in (shell_starts, pair_ids, ints, coefficients)])
    return out.reshape(2, 12, 384, 128)


def solution(mesh):
    return jax.shard_map(
        on_device,
        mesh=mesh,
        in_specs=(
            P(("coef", "pair"), None, None),
            P(None, ("coef", "pair"), None),
            P(),
            P("coef", None),
        ),
        out_specs=P(None, "pair", None, "coef"),
        check_vma=False,
    )
```

time: 118 us -> 101 us (0.86); the launches traced: 116 us -> 101 us
  Pallas kernels: 113 us -> 99.2 us
  local copies, waits for them, and re-layouts: 3.3 us -> 1.41 us
    pallas_call x1, Pallas kernels: 113 us -> 99.2 us  [on_device(): pl.pallas_call(kernel, out_shape=jax.ShapeDtypeStruct((24, 384, 128), BF1...]
    unnamed x1, local copies, waits for them, and re-layouts: 3.3 us -> 1.41 us
where the time goes in v3:
time: 101 us
  Pallas kernels  99.2 us (98%)
  local copies, waits for them, and re-layouts  1.41 us (1%)
    pallas_call x1, Pallas kernels, on_device(): pl.pallas_call(kernel, out_shape=jax.ShapeDtypeStruct((24, 384, 128), BF1...  99.2 us

profile of v3, /device:TPU:1, one launch (start us, length us, event | category | flops | bytes accessed | tf_op | source)
XLA Modules:
  0.0 100.6 jit_solution(849252644440855143)
XLA Ops:
  0.0 99.2 %shard_map.46 = bf16[24,384,128]{2,1,0:T(8,128)(2,1)S(1)} custom-call(s32[8]{0:T(128)} %starts_in.1, s32[1,128]{1,0:T(1,128)} %order_in.1, bf16[128,8192]{1,0:T(8,128)(2,1)} %bitcast.3, bf16[2,16,384]{2,1,0:T(8,128)(2,1)} %coef_ref.1), custom_call_target="tpu_custom_call" | custom-call | tf_op jit(solution)/shard_map/pallas_call | solution.py:555
  99.2 1.4 %copy.6 = bf16[2,12,384,128]{3,2,1,0:T(8,128)(2,1)} copy(bf16[2,12,384,128]{3,2,1,0:T(8,128)(2,1)S(1)} %bitcast.2) | data formatting | bytes 4718592
